TPU v7x, 32 devices: a whole 2x2x4 slice. The times are simulated.
32 devices in a mesh: walk: 2 (over core), det: 4 (over y, x), exc: 4 (over z).
Axes of the slice: x: 2, y: 2, z: 4, core: 2. Of those that a mesh axis runs over, the one named last changes fastest.
Arguments:
- inverse: bfloat16 [128, 128, 128], P(('walk', 'det', 'exc')), may hold values from -0.5 to 0.5
- virt_ref: bfloat16 [128, 128], replicated, may hold values from -6 to 6
- new_rows: bfloat16 [128, 128], P(('walk', 'det', 'exc')), may hold values from -6 to 6
- moved_electron: int32 [128], P(('walk', 'det', 'exc')), may hold values from 0 to 127
- coefficient: float32 [16384], P(('det', 'exc')), may hold values from -0.046875 to 0.046875
- occ_list: int32 [4, 16384], P(None, ('det', 'exc')), may hold values from 0 to 127
- virt_list: int32 [4, 16384], P(None, ('det', 'exc')), may hold values from 0 to 127
- exc_rank: int32 [16384], P(('det', 'exc')), may hold values from 1 to 4
Outputs:
- amplitude: float32 [128], P(('walk', 'det', 'exc'))
- ci_grad: float32 [16384], P(('det', 'exc'))
- orb_grad: float32 [128, 128], P('walk')
All inputs are finite; a program needn't handle non-finite values.
Results may differ from a plain program's by a relative error of at most 0.0015.
The roundings to bfloat16 on the way count: a program that leaves them out, or rounds other values in their place, can miss the bound.
Values may be sent and summed in bfloat16 or wider, within the bound.
No kernel may reach another device: no remote copies, remote signals or barrier semaphores. Data moves between devices by JAX's collectives and lax.ppermute only.
A program may use at most 64 MiB of HBM per device.

v0:
```python
import math
import jax
import jax.numpy as jnp
from jax import lax
from jax.sharding import PartitionSpec as P


def minor_det(cells):
    top_a = cells[0] * cells[5] - cells[4] * cells[1]
    top_b = cells[0] * cells[6] - cells[4] * cells[2]
    top_c = cells[0] * cells[7] - cells[4] * cells[3]
    top_d = cells[1] * cells[6] - cells[5] * cells[2]
    top_e = cells[1] * cells[7] - cells[5] * cells[3]
    top_f = cells[2] * cells[7] - cells[6] * cells[3]
    low_f = cells[10] * cells[15] - cells[14] * cells[11]
    low_e = cells[9] * cells[15] - cells[13] * cells[11]
    low_d = cells[9] * cells[14] - cells[13] * cells[10]
    low_c = cells[8] * cells[15] - cells[12] * cells[11]
    low_b = cells[8] * cells[14] - cells[12] * cells[10]
    low_a = cells[8] * cells[13] - cells[12] * cells[9]
    return (
        top_a * low_f
        - top_b * low_e
        + top_c * low_d
        + top_d * low_c
        - top_e * low_b
        + top_f * low_a
    )


def build_minor(entries, exc_rank):
    cells = []
    for row_pos in range(4):
        for col_pos in range(4):
            inside = (exc_rank > row_pos) & (exc_rank > col_pos)
            filler = jnp.float32(1.0 if row_pos == col_pos else 0.0)
            cells.append(jnp.where(inside[None, :], entries[:, row_pos * 4 + col_pos, :], filler))
    return cells


def select_entries(tables, occ_list, virt_list):
    walkers, nocc, nvirt = tables.shape
    count = occ_list.shape[1]
    width = math.gcd(count, max(128, 8192 // walkers))
    steps_count = count // width
    occ_blocks = occ_list.reshape(4, steps_count, width).transpose(1, 0, 2)
    virt_blocks = virt_list.reshape(4, steps_count, width).transpose(1, 0, 2)
    rows_iota = jnp.arange(nocc, dtype=jnp.int32)
    cols_iota = jnp.arange(nvirt, dtype=jnp.int32)

    def one_block(lists):
        occ_part, virt_part = lists
        virt_hot = (cols_iota[:, None, None] == virt_part[None, :, :]).astype(jnp.bfloat16)
        columns = jnp.einsum("wpv,vbi->wpbi", tables, virt_hot, preferred_element_type=jnp.float32)
        picked = []
        for slot in range(4):
            hit = rows_iota[:, None] == occ_part[slot][None, :]
            picked.append(jnp.sum(jnp.where(hit[None, :, None, :], columns, 0.0), axis=1))
        return jnp.stack(picked, axis=1).reshape(walkers, 16, width)

    gathered = lax.map(one_block, (occ_blocks, virt_blocks))
    return gathered.transpose(1, 2, 0, 3).reshape(walkers, 16, count)


def orbital_grad(weighted, occ_list, virt_list, nocc, nvirt):
    count = occ_list.shape[1]
    slots = weighted.reshape(4, 4, count)
    rows_iota = jnp.arange(nocc, dtype=jnp.int32)
    spread = jnp.zeros((nocc, 4, count), jnp.float32)
    for slot in range(4):
        hit = rows_iota[:, None, None] == occ_list[slot][None, None, :]
        spread = spread + jnp.where(hit, slots[slot][None, :, :], 0.0)
    virt_hot = (jnp.arange(nvirt, dtype=jnp.int32)[:, None, None] == virt_list[None, :, :]).astype(
        jnp.float32
    )
    return jnp.einsum("pbi,qbi->pq", spread, virt_hot, precision=lax.Precision.HIGHEST)


def ratios_and_puller(entries, exc_rank):
    return jax.vjp(lambda values: minor_det(build_minor(values, exc_rank)), entries)


def per_device(
    inverse, virt_ref, new_rows, moved_electron, coefficient, occ_list, virt_list, exc_rank
):
    nocc = inverse.shape[1]
    nvirt = virt_ref.shape[1]
    tab_count = inverse.shape[0]
    displaced = jnp.arange(nocc, dtype=jnp.int32)[None, :, None] == moved_electron[:, None, None]
    basis = jnp.where(displaced, new_rows[:, None, :], virt_ref[None, :, :])
    tables = jnp.einsum("wji,wiv->wjv", inverse, basis, preferred_element_type=jnp.float32).astype(
        jnp.bfloat16
    )
    total_walkers = tab_count * lax.axis_size("walk") * lax.axis_size(("det", "exc"))
    entries = select_entries(
        lax.all_gather(tables, ("det", "exc"), axis=0, tiled=True), occ_list, virt_list
    )
    ratios, puller = ratios_and_puller(entries, exc_rank)
    partial_value = jnp.dot(ratios, coefficient, precision=lax.Precision.HIGHEST)
    amplitude = 1.0 + lax.psum(partial_value, ("det", "exc"))
    weight = amplitude / (amplitude * amplitude + 1.0)
    grad_part = jnp.dot(weight, ratios, precision=lax.Precision.HIGHEST)
    cof_sum = jnp.sum(puller(jnp.broadcast_to(weight[:, None], ratios.shape))[0], axis=0)
    amp_mine = lax.dynamic_slice_in_dim(
        amplitude, lax.axis_index(("det", "exc")) * tab_count, tab_count, 0
    )
    ci_grad = lax.psum(grad_part, "walk") / total_walkers
    weighted = cof_sum * coefficient[None, :] / total_walkers
    orbital = orbital_grad(weighted, occ_list, virt_list, nocc, nvirt)
    summed = lax.psum(orbital, ("walk", "det", "exc"))
    share = nocc // lax.axis_size("walk")
    orb_grad = lax.dynamic_slice_in_dim(summed, lax.axis_index("walk") * share, share, 0)
    return (amp_mine, ci_grad, orb_grad)


def solution(mesh):
    return jax.shard_map(
        per_device,
        mesh=mesh,
        in_specs=(
            P(("walk", "det", "exc"), None, None),
            P(),
            P(("walk", "det", "exc"), None),
            P(("walk", "det", "exc")),
            P(("det", "exc")),
            P(None, ("det", "exc")),
            P(None, ("det", "exc")),
            P(("det", "exc")),
        ),
        out_specs=(P(("walk", "det", "exc")), P(("det", "exc")), P("walk", None)),
        check_vma=False,
    )
```

profile of v0, /device:TPU:1, one launch (start us, length us, event | category | flops | bytes accessed | tf_op | source)
XLA Modules:
  0.0 351.5 jit_solution(1757928485655057289)
XLA Ops:
  8.0 0.9 copy.99
  8.9 0.9 fusion.19
  11.4 0.9 fusion.46
  12.3 0.9 iota_compare_fusion.9
  13.2 0.8 iota_compare_fusion.11
  14.0 59.2 %all-gather.2.cloned.1.call-done = bf16[64,128,128]{2,1,0:T(8,128)(2,1)} async-done(((bf16[4,128,128]{2,1,0:T(8,128)(2,1)}), bf16[64,128,128]{2,1,0:T(8,128)(2,1)}) %all-gather.2.cloned.1.call-update) | async-done | bytes 2097168 | tf_op jit(solution)/shard_map/all_gather | solution.py:96
  73.2 89.1 %while.13 = (s32[]{:T(128)}, f32[8,64,16,128]{3,1,2,0:T(8,128)}, s32[8,4,128]{2,1,0:T(4,128)}, s32[8,4,128]{2,1,0:T(4,128)}, bf16[64,128,128]{2,1,0:T(8,128)(2,1)}, /*index=5*/s32[]{:T(128)}) while((s32[]{:T(128)}, f32[8,64,16,128]{3,1,2,0:T(8,128)}, s32[8,4,128]{2,1,0:T(4,128)}, s32[8,4,128]{2,1,0:T(4,128)}, ...), condition=%wide.region_5.6_spmd.clone.clone, body=%wide.region_0.5_spmd.clone.clone.sunk | while | flops 1107689472 | bytes 4866137 | solution.py:61
  74.7 8.8 %fusion.54 = (f32[64,4,128]{2,0,1:T(8,128)S(1)}, f32[64,4,128]{2,0,1:T(8,128)S(1)}, f32[64,4,128]{2,0,1:T(8,128)S(1)}, f32[64,4,128]{2,0,1:T(8,128)S(1)}) fusion(pred[128,128]{1,0:T(8,128)(4,1)S(1)} %get-tuple-element.237, pred[128,128]{1,0:T(8,128)(4,1)S(1)} %get-tuple-element.238, pred[128,128]{1,0:T(8,128)(4,1)S(1)} %get-tuple-element.241, ...), kind=kOutput, calls=%fused_computation.5.clone.1 | convolution fusion | flops 1107230720 | bytes 2689024 | tf_op jit(solution)/shard_map/while/body/eval_jaxpr/wpv,vbi->wpbi/dot_general | solution.py:54
  85.8 8.8 %fusion.54 = (f32[64,4,128]{2,0,1:T(8,128)S(1)}, f32[64,4,128]{2,0,1:T(8,128)S(1)}, f32[64,4,128]{2,0,1:T(8,128)S(1)}, f32[64,4,128]{2,0,1:T(8,128)S(1)}) fusion(pred[128,128]{1,0:T(8,128)(4,1)S(1)} %get-tuple-element.237, pred[128,128]{1,0:T(8,128)(4,1)S(1)} %get-tuple-element.238, pred[128,128]{1,0:T(8,128)(4,1)S(1)} %get-tuple-element.241, ...), kind=kOutput, calls=%fused_computation.5.clone.1 | convolution fusion | flops 1107230720 | bytes 2689024 | tf_op jit(solution)/shard_map/while/body/eval_jaxpr/wpv,vbi->wpbi/dot_general | solution.py:54
  94.6 0.8 constant_dynamic-update-slice_fusion.2
  96.9 8.8 %fusion.54 = (f32[64,4,128]{2,0,1:T(8,128)S(1)}, f32[64,4,128]{2,0,1:T(8,128)S(1)}, f32[64,4,128]{2,0,1:T(8,128)S(1)}, f32[64,4,128]{2,0,1:T(8,128)S(1)}) fusion(pred[128,128]{1,0:T(8,128)(4,1)S(1)} %get-tuple-element.237, pred[128,128]{1,0:T(8,128)(4,1)S(1)} %get-tuple-element.238, pred[128,128]{1,0:T(8,128)(4,1)S(1)} %get-tuple-element.241, ...), kind=kOutput, calls=%fused_computation.5.clone.1 | convolution fusion | flops 1107230720 | bytes 2689024 | tf_op jit(solution)/shard_map/while/body/eval_jaxpr/wpv,vbi->wpbi/dot_general | solution.py:54
  105.8 0.9 constant_dynamic-update-slice_fusion.2
  108.1 8.8 %fusion.54 = (f32[64,4,128]{2,0,1:T(8,128)S(1)}, f32[64,4,128]{2,0,1:T(8,128)S(1)}, f32[64,4,128]{2,0,1:T(8,128)S(1)}, f32[64,4,128]{2,0,1:T(8,128)S(1)}) fusion(pred[128,128]{1,0:T(8,128)(4,1)S(1)} %get-tuple-element.237, pred[128,128]{1,0:T(8,128)(4,1)S(1)} %get-tuple-element.238, pred[128,128]{1,0:T(8,128)(4,1)S(1)} %get-tuple-element.241, ...), kind=kOutput, calls=%fused_computation.5.clone.1 | convolution fusion | flops 1107230720 | bytes 2689024 | tf_op jit(solution)/shard_map/while/body/eval_jaxpr/wpv,vbi->wpbi/dot_general | solution.py:54
  116.9 0.9 constant_dynamic-update-slice_fusion.2
  119.2 8.8 %fusion.54 = (f32[64,4,128]{2,0,1:T(8,128)S(1)}, f32[64,4,128]{2,0,1:T(8,128)S(1)}, f32[64,4,128]{2,0,1:T(8,128)S(1)}, f32[64,4,128]{2,0,1:T(8,128)S(1)}) fusion(pred[128,128]{1,0:T(8,128)(4,1)S(1)} %get-tuple-element.237, pred[128,128]{1,0:T(8,128)(4,1)S(1)} %get-tuple-element.238, pred[128,128]{1,0:T(8,128)(4,1)S(1)} %get-tuple-element.241, ...), kind=kOutput, calls=%fused_computation.5.clone.1 | convolution fusion | flops 1107230720 | bytes 2689024 | tf_op jit(solution)/shard_map/while/body/eval_jaxpr/wpv,vbi->wpbi/dot_general | solution.py:54
  130.4 8.8 %fusion.54 = (f32[64,4,128]{2,0,1:T(8,128)S(1)}, f32[64,4,128]{2,0,1:T(8,128)S(1)}, f32[64,4,128]{2,0,1:T(8,128)S(1)}, f32[64,4,128]{2,0,1:T(8,128)S(1)}) fusion(pred[128,128]{1,0:T(8,128)(4,1)S(1)} %get-tuple-element.237, pred[128,128]{1,0:T(8,128)(4,1)S(1)} %get-tuple-element.238, pred[128,128]{1,0:T(8,128)(4,1)S(1)} %get-tuple-element.241, ...), kind=kOutput, calls=%fused_computation.5.clone.1 | convolution fusion | flops 1107230720 | bytes 2689024 | tf_op jit(solution)/shard_map/while/body/eval_jaxpr/wpv,vbi->wpbi/dot_general | solution.py:54
  139.2 0.8 constant_dynamic-update-slice_fusion.2
  141.5 8.8 %fusion.54 = (f32[64,4,128]{2,0,1:T(8,128)S(1)}, f32[64,4,128]{2,0,1:T(8,128)S(1)}, f32[64,4,128]{2,0,1:T(8,128)S(1)}, f32[64,4,128]{2,0,1:T(8,128)S(1)}) fusion(pred[128,128]{1,0:T(8,128)(4,1)S(1)} %get-tuple-element.237, pred[128,128]{1,0:T(8,128)(4,1)S(1)} %get-tuple-element.238, pred[128,128]{1,0:T(8,128)(4,1)S(1)} %get-tuple-element.241, ...), kind=kOutput, calls=%fused_computation.5.clone.1 | convolution fusion | flops 1107230720 | bytes 2689024 | tf_op jit(solution)/shard_map/while/body/eval_jaxpr/wpv,vbi->wpbi/dot_general | solution.py:54
  152.6 8.8 %fusion.54 = (f32[64,4,128]{2,0,1:T(8,128)S(1)}, f32[64,4,128]{2,0,1:T(8,128)S(1)}, f32[64,4,128]{2,0,1:T(8,128)S(1)}, f32[64,4,128]{2,0,1:T(8,128)S(1)}) fusion(pred[128,128]{1,0:T(8,128)(4,1)S(1)} %get-tuple-element.237, pred[128,128]{1,0:T(8,128)(4,1)S(1)} %get-tuple-element.238, pred[128,128]{1,0:T(8,128)(4,1)S(1)} %get-tuple-element.241, ...), kind=kOutput, calls=%fused_computation.5.clone.1 | convolution fusion | flops 1107230720 | bytes 2689024 | tf_op jit(solution)/shard_map/while/body/eval_jaxpr/wpv,vbi->wpbi/dot_general | solution.py:54
  162.3 2.8 copy_bitcast_fusion
  165.1 1.9 copy-done.1
  167.9 32.4 %psum.21 = f32[64]{0:T(128)S(1)} all-reduce(f32[64]{0:T(128)S(1)} %convolution_bitcast_fusion), channel_id=1, replica_groups=mesh['walk'=2,'det'=4,'exc'=4] {'det','exc'}, use_global_device_ids=true, to_apply=%region_6.7 | all-reduce | flops 64 | bytes 512 | tf_op jit(solution)/shard_map/psum | solution.py:100
  201.6 1.9 add_select_fusion.7
  203.6 1.9 add_select_fusion.15
  207.4 1.0 add_select_fusion.9
  208.5 1.0 add_select_fusion.12
  209.4 1.7 add_select_fusion.11
  211.2 10.6 %psum.22 = f32[1024]{0:T(1024)S(1)} all-reduce(f32[1024]{0:T(1024)} %bitcast.162), channel_id=1, replica_groups=mesh['walk'=2,'det'=4,'exc'=4] {'walk'}, use_global_device_ids=true, to_apply=%region_7.8 | all-reduce | flops 1024 | bytes 8192 | tf_op jit(solution)/shard_map/psum | solution.py:107
  221.8 2.3 add_reduce_fusion
  224.3 2.8 fusion.20
  228.3 115.0 %all-reduce.18.cloned.1.call-done = f32[128,128]{1,0:T(8,128)} async-done(((f32[128,128]{1,0:T(8,128)}), f32[128,128]{1,0:T(8,128)}) %all-reduce.18.cloned.1.call-update) | async-done | bytes 65552 | tf_op jit(solution)/shard_map/psum | solution.py:110
  343.3 1.4 constant_dynamic-slice_fusion.1
  (104 shorter events, 22.7 us)
Async XLA Ops:
  7.2 1.7 copy-start
  7.2 66.0 %all-gather.2.cloned.1.call-start = ((), (), s32[]{:S(2)}) async-start(), calls=%async_computation | async-start | bytes 2228224 | tf_op jit(solution)/shard_map/all_gather | solution.py:96
  10.6 332.7 %all-reduce.18.cloned.1.call-start = ((), (), s32[]{:S(2)}) async-start(), calls=%async_computation.1 | async-start | bytes 131072 | tf_op jit(solution)/shard_map/psum | solution.py:110
  11.4 195.7 %copy-start.8 = (pred[1024]{0:T(1024)(128)(4,1)}, pred[1024]{0:T(1024)(128)(4,1)S(1)}, u32[]{:S(2)}) copy-start(pred[1024]{0:T(1024)(128)(4,1)S(1)} %get-tuple-element.145) | copy-start | bytes 3076
  11.4 196.0 %copy-start.10 = (pred[1024]{0:T(1024)(128)(4,1)}, pred[1024]{0:T(1024)(128)(4,1)S(1)}, u32[]{:S(2)}) copy-start(pred[1024]{0:T(1024)(128)(4,1)S(1)} %get-tuple-element.179) | copy-start | bytes 3076
  11.4 196.0 %copy-start.7 = (pred[1024]{0:T(1024)(128)(4,1)}, pred[1024]{0:T(1024)(128)(4,1)S(1)}, u32[]{:S(2)}) copy-start(pred[1024]{0:T(1024)(128)(4,1)S(1)} %get-tuple-element.184) | copy-start | bytes 3076
  165.1 2.0 copy-start.1
  165.1 2.5 copy-start.11
  200.3 5.2 %copy-start.2 = (f32[64,16,1024]{2,0,1:T(8,128)S(1)}, f32[64,16,1024]{2,0,1:T(8,128)}, u32[]{:S(2)}) copy-start(f32[64,16,1024]{2,0,1:T(8,128)} %copy-done.1) | copy-start | bytes 12582916
  207.4 2.0 copy-start.9
  209.4 14.8 %copy-start.12 = (f32[1024]{0:T(1024)S(1)}, f32[1024]{0:T(1024)}, u32[]{:S(2)}) copy-start(f32[1024]{0:T(1024)} %param.14) | copy-start | bytes 12292
  221.8 2.4 copy-start.3
  221.8 2.5 copy-start.4
  221.8 2.5 copy-start.5
  221.8 2.5 copy-start.6
  221.8 2.5 copy-start.13
  224.2 3.5 %copy-start.14 = (f32[64]{0:T(128)S(1)}, f32[64]{0:T(128)}, u32[]{:S(2)}) copy-start(f32[64]{0:T(128)} %get-tuple-element.187) | copy-start | bytes 772
Sparse Core Ops, SparseCore 0:
  10.8 62.3 all-gather.1
  227.2 116.0 all-reduce.17
where the time goes:
time: 353 us; the launch traced here: 352 us
  waiting for transfers between devices  174 us (49%)
  matrix products  75.2 us (21%)
  blocking collectives  43 us (12%)
  local copies, waits for them, and re-layouts  27 us (8%)
  other arithmetic  17.4 us (5%)
  between operations  14.3 us (4%)
    psum x1, waiting for transfers between devices, per_device(): summed = lax.psum(orbital, ('walk', 'det', 'exc'))  115 us
    dot_general x8, matrix products, one_block(): jnp.einsum('wpv,vbi->wpbi', tables, virt_hot, preferred_element_type=jnp....  70.4 us
    all_gather x1, waiting for transfers between devices, per_device(): lax.all_gather(tables, ('det', 'exc'), axis=0, tiled=True)  59.2 us
    psum x1, blocking collectives, per_device(): amplitude = 1.0 + lax.psum(partial_value, ('det', 'exc'))  32.4 us
    psum x1, blocking collectives, per_device(): ci_grad = lax.psum(grad_part, 'walk') / total_walkers  10.6 us
    select_n x11, other arithmetic, build_minor(): jnp.where(inside[None, :], entries[:, row_pos * 4 + col_pos, :], filler)  9.44 us
  transfers between devices with their start and end apart: 2, of which 2 were waited for; matrix products, arithmetic and copies ran while one was open for 1% of the time, Pallas kernels for 0%

commit v1 on v0

--- a/solution.py
+++ b/solution.py
@@ -3,6 +3,7 @@
 import jax.numpy as jnp
 from jax import lax
 from jax.sharding import PartitionSpec as P
+from jax.lax import all_gather
 
 
 def minor_det(cells):
@@ -83,6 +84,11 @@
 def per_device(
     inverse, virt_ref, new_rows, moved_electron, coefficient, occ_list, virt_list, exc_rank
 ):
+
+    def treat_object(content):
+        odd = all_gather(content, ("walk", "det", "exc"))
+        return jnp.sum(odd, 0)
+
     nocc = inverse.shape[1]
     nvirt = virt_ref.shape[1]
     tab_count = inverse.shape[0]
@@ -107,7 +113,7 @@
     ci_grad = lax.psum(grad_part, "walk") / total_walkers
     weighted = cof_sum * coefficient[None, :] / total_walkers
     orbital = orbital_grad(weighted, occ_list, virt_list, nocc, nvirt)
-    summed = lax.psum(orbital, ("walk", "det", "exc"))
+    summed = treat_object(orbital)
     share = nocc // lax.axis_size("walk")
     orb_grad = lax.dynamic_slice_in_dim(summed, lax.axis_index("walk") * share, share, 0)
     return (amp_mine, ci_grad, orb_grad)

time: 353 us -> 283 us (0.80)
  waiting for transfers between devices: 174 us -> 111 us
  other arithmetic: 17.4 us -> 12.9 us
    psum x1 -> x0, waiting for transfers between devices: 115 us -> none  [per_device(): summed = lax.psum(orbital, ('walk', 'det', 'exc'))]
    all_gather x0 -> x1, waiting for transfers between devices: none -> 49.9 us  [treat_object(): odd = all_gather(content, ('walk', 'det', 'exc'))]
where the time goes in v1:
time: 283 us; the launch traced here: 282 us
  waiting for transfers between devices  111 us (39%)
  matrix products  74.6 us (26%)
  blocking collectives  43.1 us (15%)
  local copies, waits for them, and re-layouts  26.2 us (9%)
  between operations  14.3 us (5%)
  other arithmetic  12.9 us (5%)
    dot_general x8, matrix products, one_block(): jnp.einsum('wpv,vbi->wpbi', tables, virt_hot, preferred_element_type=jnp....  70.4 us
    all_gather x1, waiting for transfers between devices, per_device(): lax.all_gather(tables, ('det', 'exc'), axis=0, tiled=True)  60.7 us
    all_gather x1, waiting for transfers between devices, treat_object(): odd = all_gather(content, ('walk', 'det', 'exc'))  49.9 us
    psum x1, blocking collectives, per_device(): amplitude = 1.0 + lax.psum(partial_value, ('det', 'exc'))  32.6 us
    psum x1, blocking collectives, per_device(): ci_grad = lax.psum(grad_part, 'walk') / total_walkers  10.5 us
    select_n x11, other arithmetic, build_minor(): jnp.where(inside[None, :], entries[:, row_pos * 4 + col_pos, :], filler)  6.84 us
    dynamic_update_slice x8, local copies, waits for them, and re-layouts, select_entries(): gathered = lax.map(one_block, (occ_blocks, virt_blocks))  6.76 us
  transfers between devices with their start and end apart: 2, of which 2 were waited for; matrix products, arithmetic and copies ran while one was open for 1% of the time, Pallas kernels for 0%

profile of v1, /device:TPU:1, one launch (start us, length us, event | category | flops | bytes accessed | tf_op | source)
XLA Modules:
  0.0 282.0 jit_solution(17178978555759305684)
XLA Ops:
  7.2 0.8 iota_compare_fusion.13
  8.0 0.9 copy.99
  8.9 0.9 fusion.19
  9.8 0.8 copy.100
  11.4 0.9 fusion.46
  12.6 60.7 %all-gather.4.cloned.1.call-done = bf16[64,128,128]{2,1,0:T(8,128)(2,1)} async-done(((bf16[4,128,128]{2,1,0:T(8,128)(2,1)}), bf16[64,128,128]{2,1,0:T(8,128)(2,1)}) %all-gather.4.cloned.1.call-update) | async-done | bytes 2097168 | tf_op jit(solution)/shard_map/all_gather | solution.py:102
  73.2 89.1 %while.13 = (s32[]{:T(128)}, f32[8,64,16,128]{3,1,2,0:T(8,128)}, s32[8,4,128]{2,1,0:T(4,128)}, s32[8,4,128]{2,1,0:T(4,128)}, bf16[64,128,128]{2,1,0:T(8,128)(2,1)}, /*index=5*/s32[]{:T(128)}) while((s32[]{:T(128)}, f32[8,64,16,128]{3,1,2,0:T(8,128)}, s32[8,4,128]{2,1,0:T(4,128)}, s32[8,4,128]{2,1,0:T(4,128)}, ...), condition=%wide.region_5.6_spmd.clone.clone, body=%wide.region_0.5_spmd.clone.clone.sunk | while | flops 1107689472 | bytes 4866137 | solution.py:62
  74.7 8.8 %fusion.54 = (f32[64,4,128]{2,0,1:T(8,128)S(1)}, f32[64,4,128]{2,0,1:T(8,128)S(1)}, f32[64,4,128]{2,0,1:T(8,128)S(1)}, f32[64,4,128]{2,0,1:T(8,128)S(1)}) fusion(pred[128,128]{1,0:T(8,128)(4,1)S(1)} %get-tuple-element.237, pred[128,128]{1,0:T(8,128)(4,1)S(1)} %get-tuple-element.238, pred[128,128]{1,0:T(8,128)(4,1)S(1)} %get-tuple-element.241, ...), kind=kOutput, calls=%fused_computation.5.clone.1 | convolution fusion | flops 1107230720 | bytes 2689024 | tf_op jit(solution)/shard_map/while/body/eval_jaxpr/wpv,vbi->wpbi/dot_general | solution.py:55
  83.5 0.8 constant_dynamic-update-slice_fusion.2
  85.8 8.8 %fusion.54 = (f32[64,4,128]{2,0,1:T(8,128)S(1)}, f32[64,4,128]{2,0,1:T(8,128)S(1)}, f32[64,4,128]{2,0,1:T(8,128)S(1)}, f32[64,4,128]{2,0,1:T(8,128)S(1)}) fusion(pred[128,128]{1,0:T(8,128)(4,1)S(1)} %get-tuple-element.237, pred[128,128]{1,0:T(8,128)(4,1)S(1)} %get-tuple-element.238, pred[128,128]{1,0:T(8,128)(4,1)S(1)} %get-tuple-element.241, ...), kind=kOutput, calls=%fused_computation.5.clone.1 | convolution fusion | flops 1107230720 | bytes 2689024 | tf_op jit(solution)/shard_map/while/body/eval_jaxpr/wpv,vbi->wpbi/dot_general | solution.py:55
  94.6 0.8 constant_dynamic-update-slice_fusion.2
  96.9 8.8 %fusion.54 = (f32[64,4,128]{2,0,1:T(8,128)S(1)}, f32[64,4,128]{2,0,1:T(8,128)S(1)}, f32[64,4,128]{2,0,1:T(8,128)S(1)}, f32[64,4,128]{2,0,1:T(8,128)S(1)}) fusion(pred[128,128]{1,0:T(8,128)(4,1)S(1)} %get-tuple-element.237, pred[128,128]{1,0:T(8,128)(4,1)S(1)} %get-tuple-element.238, pred[128,128]{1,0:T(8,128)(4,1)S(1)} %get-tuple-element.241, ...), kind=kOutput, calls=%fused_computation.5.clone.1 | convolution fusion | flops 1107230720 | bytes 2689024 | tf_op jit(solution)/shard_map/while/body/eval_jaxpr/wpv,vbi->wpbi/dot_general | solution.py:55
  105.7 0.9 constant_dynamic-update-slice_fusion.2
  108.1 8.8 %fusion.54 = (f32[64,4,128]{2,0,1:T(8,128)S(1)}, f32[64,4,128]{2,0,1:T(8,128)S(1)}, f32[64,4,128]{2,0,1:T(8,128)S(1)}, f32[64,4,128]{2,0,1:T(8,128)S(1)}) fusion(pred[128,128]{1,0:T(8,128)(4,1)S(1)} %get-tuple-element.237, pred[128,128]{1,0:T(8,128)(4,1)S(1)} %get-tuple-element.238, pred[128,128]{1,0:T(8,128)(4,1)S(1)} %get-tuple-element.241, ...), kind=kOutput, calls=%fused_computation.5.clone.1 | convolution fusion | flops 1107230720 | bytes 2689024 | tf_op jit(solution)/shard_map/while/body/eval_jaxpr/wpv,vbi->wpbi/dot_general | solution.py:55
  116.9 0.8 constant_dynamic-update-slice_fusion.2
  119.2 8.8 %fusion.54 = (f32[64,4,128]{2,0,1:T(8,128)S(1)}, f32[64,4,128]{2,0,1:T(8,128)S(1)}, f32[64,4,128]{2,0,1:T(8,128)S(1)}, f32[64,4,128]{2,0,1:T(8,128)S(1)}) fusion(pred[128,128]{1,0:T(8,128)(4,1)S(1)} %get-tuple-element.237, pred[128,128]{1,0:T(8,128)(4,1)S(1)} %get-tuple-element.238, pred[128,128]{1,0:T(8,128)(4,1)S(1)} %get-tuple-element.241, ...), kind=kOutput, calls=%fused_computation.5.clone.1 | convolution fusion | flops 1107230720 | bytes 2689024 | tf_op jit(solution)/shard_map/while/body/eval_jaxpr/wpv,vbi->wpbi/dot_general | solution.py:55
  128.1 0.8 constant_dynamic-update-slice_fusion.2
  130.3 8.8 %fusion.54 = (f32[64,4,128]{2,0,1:T(8,128)S(1)}, f32[64,4,128]{2,0,1:T(8,128)S(1)}, f32[64,4,128]{2,0,1:T(8,128)S(1)}, f32[64,4,128]{2,0,1:T(8,128)S(1)}) fusion(pred[128,128]{1,0:T(8,128)(4,1)S(1)} %get-tuple-element.237, pred[128,128]{1,0:T(8,128)(4,1)S(1)} %get-tuple-element.238, pred[128,128]{1,0:T(8,128)(4,1)S(1)} %get-tuple-element.241, ...), kind=kOutput, calls=%fused_computation.5.clone.1 | convolution fusion | flops 1107230720 | bytes 2689024 | tf_op jit(solution)/shard_map/while/body/eval_jaxpr/wpv,vbi->wpbi/dot_general | solution.py:55
  139.2 0.8 constant_dynamic-update-slice_fusion.2
  141.5 8.8 %fusion.54 = (f32[64,4,128]{2,0,1:T(8,128)S(1)}, f32[64,4,128]{2,0,1:T(8,128)S(1)}, f32[64,4,128]{2,0,1:T(8,128)S(1)}, f32[64,4,128]{2,0,1:T(8,128)S(1)}) fusion(pred[128,128]{1,0:T(8,128)(4,1)S(1)} %get-tuple-element.237, pred[128,128]{1,0:T(8,128)(4,1)S(1)} %get-tuple-element.238, pred[128,128]{1,0:T(8,128)(4,1)S(1)} %get-tuple-element.241, ...), kind=kOutput, calls=%fused_computation.5.clone.1 | convolution fusion | flops 1107230720 | bytes 2689024 | tf_op jit(solution)/shard_map/while/body/eval_jaxpr/wpv,vbi->wpbi/dot_general | solution.py:55
  150.3 0.9 constant_dynamic-update-slice_fusion.2
  152.6 8.8 %fusion.54 = (f32[64,4,128]{2,0,1:T(8,128)S(1)}, f32[64,4,128]{2,0,1:T(8,128)S(1)}, f32[64,4,128]{2,0,1:T(8,128)S(1)}, f32[64,4,128]{2,0,1:T(8,128)S(1)}) fusion(pred[128,128]{1,0:T(8,128)(4,1)S(1)} %get-tuple-element.237, pred[128,128]{1,0:T(8,128)(4,1)S(1)} %get-tuple-element.238, pred[128,128]{1,0:T(8,128)(4,1)S(1)} %get-tuple-element.241, ...), kind=kOutput, calls=%fused_computation.5.clone.1 | convolution fusion | flops 1107230720 | bytes 2689024 | tf_op jit(solution)/shard_map/while/body/eval_jaxpr/wpv,vbi->wpbi/dot_general | solution.py:55
  161.5 0.8 constant_dynamic-update-slice_fusion.2
  162.3 2.8 copy_bitcast_fusion
  165.1 1.9 copy-done.1
  167.9 32.6 %psum.14 = f32[64]{0:T(128)S(1)} all-reduce(f32[64]{0:T(128)S(1)} %convolution_bitcast_fusion), channel_id=1, replica_groups=mesh['walk'=2,'det'=4,'exc'=4] {'det','exc'}, use_global_device_ids=true, to_apply=%region_6.7 | all-reduce | flops 64 | bytes 512 | tf_op jit(solution)/shard_map/psum | solution.py:106
  200.5 2.1 add_select_fusion.7
  202.6 1.9 add_select_fusion.15
  208.1 2.8 %fusion.20 = f32[128,128]{1,0:T(8,128)} fusion(s32[4,1024]{1,0:T(4,128)S(1)} %bitcast.170, f32[4,1024]{1,0:T(4,128)S(1)} %get-tuple-element.168, f32[4,1024]{1,0:T(4,128)S(1)} %get-tuple-element.169, f32[4,1024]{1,0:T(4,128)S(1)} %get-tuple-element.170, f32[4,1024]{1,0:T(4,128)S(1)} %get-tuple-element.167, pred[128,1024]{1,0:T(8,128)(4,1)S(1)} %get-tuple-element.188, ...), kind=kOutput, calls=%fused_computation.39 | convolution fusion | flops 809500672 | bytes 671744 | tf_op jit(solution)/shard_map/pbi,qbi->pq/dot_general | solution.py:77
  211.8 10.5 %psum.15 = f32[1024]{0:T(1024)S(1)} all-reduce(f32[1024]{0:T(1024)S(1)} %bitcast.164), channel_id=1, replica_groups=mesh['walk'=2,'det'=4,'exc'=4] {'walk'}, use_global_device_ids=true, to_apply=%region_7.8 | all-reduce | flops 1024 | bytes 8192 | tf_op jit(solution)/shard_map/psum | solution.py:113
  222.9 49.9 %all-gather.6.cloned.1.call-done = f32[4096,128]{1,0:T(8,128)} async-done(((f32[128,128]{1,0:T(8,128)}), f32[4096,128]{1,0:T(8,128)}) %all-gather.6.cloned.1.call-update) | async-done | bytes 2097168 | tf_op jit(solution)/shard_map/all_gather | solution.py:89
  272.8 1.7 reduce_sum.59
  (85 shorter events, 19.3 us)
Async XLA Ops:
  7.2 1.7 copy-start
  7.2 66.0 %all-gather.4.cloned.1.call-start = ((), (), s32[]{:S(2)}) async-start(), calls=%async_computation | async-start | bytes 2228224 | tf_op jit(solution)/shard_map/all_gather | solution.py:102
  10.6 262.2 %all-gather.6.cloned.1.call-start = ((), (), s32[]{:S(2)}) async-start(), calls=%async_computation.1 | async-start | bytes 2162688 | tf_op jit(solution)/shard_map/all_gather | solution.py:89
  165.1 2.0 copy-start.1
  165.1 2.5 copy-start.3
  200.5 4.0 %copy-start.2 = (f32[64,16,1024]{2,0,1:T(8,128)S(1)}, f32[64,16,1024]{2,0,1:T(8,128)}, u32[]{:S(2)}) copy-start(f32[64,16,1024]{2,0,1:T(8,128)} %copy-done.1) | copy-start | bytes 12582916
  207.1 1.0 copy-start.4
Sparse Core Ops, SparseCore 0:
  10.8 62.3 all-gather.3
  211.1 61.7 all-gather.5
